TPU v7x, 128 devices: a whole 4x4x4 slice. The times are simulated.
128 devices in a mesh: seq: 16 (over z, y_hi, core), chan: 8 (over y_lo, x).
Axes of the slice: x: 4, y: 4 (y_hi: 2, y_lo: 2; y = y_hi * 2 + y_lo), z: 4, core: 2. Of those that a mesh axis runs over, the one named last changes fastest.
Arguments:
- values: bfloat16 [4096, 4096], P('seq', 'chan'), may hold values from -6 to 6
- gates: bfloat16 [4096, 4096], P('seq', 'chan'), may hold values from -6 to 6
- filters: bfloat16 [1024, 4096], P(None, 'chan'), may hold values from -2 to 2
- skip: float32 [4096], P('chan'), may hold values from -4 to 4
- out_weight: bfloat16 [4096, 4096], P(('seq', 'chan')), may hold values from -0.09375 to 0.09375
Outputs:
- projected: bfloat16 [4096, 4096], P(('seq', 'chan'))
All inputs are finite; a program needn't handle non-finite values.
Results may differ from a plain program's by a relative error of at most 0.009.
Values may be sent and summed in bfloat16 or wider, within the bound.
A program may use at most 128 MiB of HBM per device.

v0:
```python
import numpy as np
import jax
import jax.numpy as jnp
from jax import lax
from jax.sharding import PartitionSpec as P


def dft_tables(block):
    size = 2 * block
    freq = (np.arange(block) + 0.5)[:, None]
    angle = 2.0 * np.pi * freq * np.arange(size)[None, :] / size
    forward = np.concatenate([np.cos(angle), -np.sin(angle)], axis=0)
    late = angle[:, block:]
    backward = np.concatenate([np.cos(late), -np.sin(late)], axis=0).T / block
    return (forward, backward)


def from_behind(value, axis, steps):
    count = lax.axis_size(axis)
    return lax.ppermute(value, axis, [(source, source + steps) for source in range(count - steps)])


def dot(a, b):
    return jnp.dot(a, b, preferred_element_type=jnp.float32)


def body(values, gates, filters, skip, out_weight):
    block = values.shape[0]
    taps = filters.shape[0] // block
    forward, backward = dft_tables(block)
    forward = jnp.asarray(forward, jnp.bfloat16)
    backward = jnp.asarray(backward, jnp.bfloat16)
    part = lax.all_to_all(out_weight, "chan", split_axis=1, concat_axis=0, tiled=True)
    columns = lax.all_gather(part, "seq", axis=0, tiled=True)
    blocks = [values] + [from_behind(values, "seq", step) for step in range(1, taps + 1)]
    real = 0.0
    imag = 0.0
    for j in range(taps):
        kernel = dot(forward[:, :block], filters[j * block : (j + 1) * block])
        window = dot(forward, jnp.concatenate([blocks[j + 1], blocks[j]], axis=0))
        kr, ki = (kernel[:block], kernel[block:])
        wr, wi = (window[:block], window[block:])
        real = real + kr * wr - ki * wi
        imag = imag + kr * wi + ki * wr
    spectrum = jnp.concatenate([real, imag], axis=0).astype(jnp.bfloat16)
    filtered = dot(backward, spectrum) + skip[None, :] * values.astype(jnp.float32)
    gated = (gates.astype(jnp.float32) * filtered).astype(jnp.bfloat16)
    rows = lax.all_gather(gated, "chan", axis=1, tiled=True)
    summed = dot(rows, columns).astype(jnp.bfloat16)
    return lax.all_to_all(summed, "chan", split_axis=0, concat_axis=1, tiled=True)


def solution(mesh):
    in_specs = (
        P("seq", "chan"),
        P("seq", "chan"),
        P(None, "chan"),
        P("chan"),
        P(("seq", "chan"), None),
    )
    out_specs = P(("seq", "chan"), None)
    return jax.shard_map(body, mesh=mesh, in_specs=in_specs, out_specs=out_specs, check_vma=False)
```

profile of v0, /device:TPU:1, one launch (start us, length us, event | category | flops | bytes accessed | tf_op | source)
XLA Modules:
  0.0 166.8 jit_solution(8608560338992499461)
XLA Ops:
  6.5 6.5 %collective-permute-start.1 = (bf16[256,512]{1,0:T(8,128)(2,1)}, bf16[256,512]{1,0:T(8,128)(2,1)}, u32[]{:S(2)}, u32[]{:S(2)}) collective-permute-start(bf16[256,512]{1,0:T(8,128)(2,1)} %param.7), channel_id=1, source_target_pairs={{0,16},{8,24},{16,32},{24,40},{32,48},{40,56},{48,64},{56,72},{64,... | collective-permute-start | bytes 786440 | tf_op jit(solution)/shard_map/ppermute | solution.py:20
  13.0 4.4 %collective-permute-start.2 = (bf16[256,512]{1,0:T(8,128)(2,1)}, bf16[256,512]{1,0:T(8,128)(2,1)}, u32[]{:S(2)}, u32[]{:S(2)}) collective-permute-start(bf16[256,512]{1,0:T(8,128)(2,1)} %param.7), channel_id=1, source_target_pairs={{0,24},{8,32},{16,40},{24,48},{32,56},{40,64},{48,72},{56,80},{64,... | collective-permute-start | bytes 786440 | tf_op jit(solution)/shard_map/ppermute | solution.py:20
  17.4 4.0 %collective-permute-start = (bf16[256,512]{1,0:T(8,128)(2,1)}, bf16[256,512]{1,0:T(8,128)(2,1)}, u32[]{:S(2)}, u32[]{:S(2)}) collective-permute-start(bf16[256,512]{1,0:T(8,128)(2,1)} %param.7), channel_id=1, source_target_pairs={{0,8},{8,16},{16,24},{24,32},{32,40},{40,48},{48,56},{56,64},{64,7... | collective-permute-start | bytes 786440 | tf_op jit(solution)/shard_map/ppermute | solution.py:20
  21.4 3.6 %collective-permute-start.3 = (bf16[256,512]{1,0:T(8,128)(2,1)}, bf16[256,512]{1,0:T(8,128)(2,1)}, u32[]{:S(2)}, u32[]{:S(2)}) collective-permute-start(bf16[256,512]{1,0:T(8,128)(2,1)} %param.7), channel_id=1, source_target_pairs={{0,32},{8,40},{16,48},{24,56},{32,64},{40,72},{48,80},{56,88},{64,... | collective-permute-start | bytes 786440 | tf_op jit(solution)/shard_map/ppermute | solution.py:20
  25.0 1.3 fusion.10
  26.3 1.3 fusion.4
  27.6 1.3 fusion.6
  29.0 2.2 %fusion.8 = f32[512,512]{1,0:T(8,128)} fusion(bf16[512,256]{1,0:T(8,128)(2,1)S(1)} %copy-done, bf16[1024,512]{1,0:T(8,128)(2,1)} %param.9), kind=kOutput, calls=%fused_computation.17 | convolution fusion | flops 134217728 | bytes 1572864 | tf_op jit(solution)/shard_map/dot_general | solution.py:24
  31.2 1.8 %copy.15 = bf16[256,512]{0,1:T(8,128)(2,1)} copy(bf16[256,512]{1,0:T(8,128)(2,1)} %param.7) | data formatting | bytes 524288 | tf_op args[0]
  33.0 1.8 %copy.14 = bf16[256,512]{0,1:T(8,128)(2,1)} copy(bf16[256,512]{1,0:T(8,128)(2,1)} %param.8) | data formatting | bytes 524288 | tf_op args[1]
  34.8 1.4 fusion.13
  36.2 1.2 convolution_add_fusion.3
  37.4 1.2 fusion.14
  38.7 1.2 convolution_add_fusion.2
  39.9 0.0 copy-start.7
  40.0 1.3 fusion.15
  41.3 1.2 convolution_add_fusion.1
  42.6 0.0 copy-start.6
  42.6 0.0 copy-start.8
  42.6 1.3 fusion.16
  43.9 1.2 convolution_add_fusion
  45.2 1.0 fusion.12
  46.2 1.7 %fusion.3 = bf16[256,512]{0,1:T(8,128)(2,1)} fusion(f32[512,256]{1,0:T(8,128)S(1)} %fusion.12, bf16[256,256]{1,0:T(8,128)(2,1)S(1)} %copy-done.6, bf16[256,512]{0,1:T(8,128)(2,1)S(1)} %copy-done.3, bf16[256,512]{0,1:T(8,128)(2,1)S(1)} %copy-done.4, f32[512]{0:T(512)S(1)} %copy-done.8, f32[512,512]{1,0:T(8,128)S(1)} %convolution_add_fusion, ...), kind=kOutput, calls=%fused_computation.8 | convolution fusion | flops 70123520 | bytes 9832448 | tf_op jit(solution)/shard_map/dot_general | solution.py:24
  47.9 0.0 all-gather.3.cloned.1.call-update
  48.0 0.0 all-gather.5.cloned.1.call-start
  48.0 12.4 %all_to_all.38 = bf16[32,8,512]{2,0,1:T(8,128)(2,1)} all-to-all(bf16[32,8,512]{2,0,1:T(8,128)(2,1)S(1)} %bitcast.45), channel_id=1, replica_groups=mesh['seq'=16,'chan'=8] {'chan'}, dimensions={1} | all-to-all | bytes 524288 | tf_op jit(solution)/shard_map/all_to_all | solution.py:33
  60.4 0.0 all-gather.5.cloned.1.call-update
  60.5 22.0 %all-gather.3.cloned.1.call-done = bf16[256,4096]{0,1:T(8,128)(2,1)} async-done(((bf16[256,512]{0,1:T(8,128)(2,1)}), bf16[256,4096]{0,1:T(8,128)(2,1)}) %all-gather.3.cloned.1.call-update) | async-done | bytes 2097168 | tf_op jit(solution)/shard_map/all_gather | solution.py:48
  82.5 61.5 %all-gather.5.cloned.1.call-done = bf16[4096,512]{1,0:T(8,128)(2,1)} async-done(((bf16[256,512]{1,0:T(8,128)(2,1)}), bf16[4096,512]{1,0:T(8,128)(2,1)}) %all-gather.5.cloned.1.call-update) | async-done | bytes 4194320 | tf_op jit(solution)/shard_map/all_gather | solution.py:34
  144.0 4.1 %convolution_convert_fusion = bf16[256,512]{1,0:T(8,128)(2,1)S(1)} fusion(bf16[256,4096]{0,1:T(8,128)(2,1)} %all-gather.3.cloned.1.call-done, bf16[4096,512]{1,0:T(8,128)(2,1)} %all-gather.5.cloned.1.call-done), kind=kOutput, calls=%fused_computation.9 | convolution fusion | flops 1073872896 | bytes 6553600 | tf_op jit(solution)/shard_map/dot_general | solution.py:24
  148.0 11.2 %all_to_all.39 = bf16[8,32,512]{2,1,0:T(8,128)(2,1)S(1)} all-to-all(bf16[8,32,512]{2,1,0:T(8,128)(2,1)S(1)} %bitcast.47), channel_id=1, replica_groups=mesh['seq'=16,'chan'=8] {'chan'}, dimensions={0} | all-to-all | bytes 524288 | tf_op jit(solution)/shard_map/all_to_all | solution.py:50
  159.3 0.7 copy.19
  (21 shorter events, 0.1 us)
Async XLA Ops:
  6.5 22.4 %copy-start = (bf16[512,256]{1,0:T(8,128)(2,1)S(1)}, bf16[512,256]{1,0:T(8,128)(2,1)}, u32[]{:S(2)}) copy-start(bf16[512,256]{1,0:T(8,128)(2,1)} %constant.7) | copy-start | bytes 786436
  6.5 75.9 %all-gather.3.cloned.1.call-start = ((), (), s32[]{:S(2)}) async-start(), calls=%async_computation.2 | async-start | bytes 2359296 | tf_op jit(solution)/shard_map/all_gather | solution.py:48
  6.5 32.1 %collective-permute-start.1 = (bf16[256,512]{1,0:T(8,128)(2,1)}, bf16[256,512]{1,0:T(8,128)(2,1)}, u32[]{:S(2)}, u32[]{:S(2)}) collective-permute-start(bf16[256,512]{1,0:T(8,128)(2,1)} %param.7), channel_id=1, source_target_pairs={{0,16},{8,24},{16,32},{24,40},{32,48},{40,56},{48,64},{56,72},{64,... | collective-permute-start | bytes 786440 | tf_op jit(solution)/shard_map/ppermute | solution.py:20
  13.0 28.3 %collective-permute-start.2 = (bf16[256,512]{1,0:T(8,128)(2,1)}, bf16[256,512]{1,0:T(8,128)(2,1)}, u32[]{:S(2)}, u32[]{:S(2)}) collective-permute-start(bf16[256,512]{1,0:T(8,128)(2,1)} %param.7), channel_id=1, source_target_pairs={{0,24},{8,32},{16,40},{24,48},{32,56},{40,64},{48,72},{56,80},{64,... | collective-permute-start | bytes 786440 | tf_op jit(solution)/shard_map/ppermute | solution.py:20
  17.4 18.8 %collective-permute-start = (bf16[256,512]{1,0:T(8,128)(2,1)}, bf16[256,512]{1,0:T(8,128)(2,1)}, u32[]{:S(2)}, u32[]{:S(2)}) collective-permute-start(bf16[256,512]{1,0:T(8,128)(2,1)} %param.7), channel_id=1, source_target_pairs={{0,8},{8,16},{16,24},{24,32},{32,40},{40,48},{48,56},{56,64},{64,7... | collective-permute-start | bytes 786440 | tf_op jit(solution)/shard_map/ppermute | solution.py:20
  21.4 22.5 %collective-permute-start.3 = (bf16[256,512]{1,0:T(8,128)(2,1)}, bf16[256,512]{1,0:T(8,128)(2,1)}, u32[]{:S(2)}, u32[]{:S(2)}) collective-permute-start(bf16[256,512]{1,0:T(8,128)(2,1)} %param.7), channel_id=1, source_target_pairs={{0,32},{8,40},{16,48},{24,56},{32,64},{40,72},{48,80},{56,88},{64,... | collective-permute-start | bytes 786440 | tf_op jit(solution)/shard_map/ppermute | solution.py:20
  34.8 2.6 %copy-start.2 = (bf16[512,256]{1,0:T(8,128)(2,1)S(1)}, bf16[512,256]{1,0:T(8,128)(2,1)}, u32[]{:S(2)}) copy-start(bf16[512,256]{1,0:T(8,128)(2,1)} %constant.8) | copy-start | bytes 786436
  39.9 5.2 %copy-start.1 = (f32[512,512]{1,0:T(8,128)S(1)}, f32[512,512]{1,0:T(8,128)}, u32[]{:S(2)}) copy-start(f32[512,512]{1,0:T(8,128)} %fusion.8) | copy-start | bytes 3145732
  39.9 5.2 %copy-start.7 = (bf16[256,256]{1,0:T(8,128)(2,1)S(1)}, bf16[256,256]{1,0:T(8,128)(2,1)}, u32[]{:S(2)}) copy-start(bf16[256,256]{1,0:T(8,128)(2,1)} %constant.9) | copy-start | bytes 393220
  42.6 3.6 %copy-start.3 = (bf16[256,512]{0,1:T(8,128)(2,1)S(1)}, bf16[256,512]{0,1:T(8,128)(2,1)}, u32[]{:S(2)}) copy-start(bf16[256,512]{0,1:T(8,128)(2,1)} %copy.15) | copy-start | bytes 786436
  42.6 3.6 %copy-start.4 = (bf16[256,512]{0,1:T(8,128)(2,1)S(1)}, bf16[256,512]{0,1:T(8,128)(2,1)}, u32[]{:S(2)}) copy-start(bf16[256,512]{0,1:T(8,128)(2,1)} %copy.14) | copy-start | bytes 786436
  42.6 3.6 %copy-start.6 = (bf16[256,256]{1,0:T(8,128)(2,1)S(1)}, bf16[256,256]{1,0:T(8,128)(2,1)}, u32[]{:S(2)}) copy-start(bf16[256,256]{1,0:T(8,128)(2,1)} %constant.10) | copy-start | bytes 393220
  42.6 3.6 %copy-start.8 = (f32[512]{0:T(512)S(1)}, f32[512]{0:T(512)}, u32[]{:S(2)}) copy-start(f32[512]{0:T(512)} %param.10) | copy-start | bytes 6148
  45.2 2.8 %copy-start.5 = (bf16[32,4096]{1,0:T(8,128)(2,1)S(1)}, bf16[32,4096]{1,0:T(8,128)(2,1)}, u32[]{:S(2)}) copy-start(bf16[32,4096]{1,0:T(8,128)(2,1)} %param.11) | copy-start | bytes 786436
  48.0 96.0 %all-gather.5.cloned.1.call-start = ((), (), s32[]{:S(2)}) async-start(), calls=%async_computation.3 | async-start | bytes 4456448 | tf_op jit(solution)/shard_map/all_gather | solution.py:34
Sparse Core Ops, SparseCore 0:
  48.1 34.3 all-gather.2
  84.9 58.9 all-gather.4
where the time goes:
time: 167 us
  waiting for transfers between devices  83.5 us (50%)
  blocking collectives  23.6 us (14%)
  matrix products  23.1 us (14%)
  starting transfers between devices  18.5 us (11%)
  between operations  13.6 us (8%)
  local copies, waits for them, and re-layouts  4.39 us (3%)
    all_gather x1, waiting for transfers between devices, body(): columns = lax.all_gather(part, 'seq', axis=0, tiled=True)  61.5 us
    dot_general x15, matrix products, dot(): return jnp.dot(a, b, preferred_element_type=jnp.float32)  23.1 us
    all_gather x1, waiting for transfers between devices, body(): rows = lax.all_gather(gated, 'chan', axis=1, tiled=True)  22 us
    ppermute x4, starting transfers between devices, from_behind(): lax.ppermute(value, axis, [(source, source + steps) for source in range(c...  18.5 us
    all_to_all x1, blocking collectives, body(): lax.all_to_all(out_weight, 'chan', split_axis=1, concat_axis=0, tiled=True)  12.4 us
    all_to_all x1, blocking collectives, body(): lax.all_to_all(summed, 'chan', split_axis=0, concat_axis=1, tiled=True)  11.2 us
    unnamed x20, local copies, waits for them, and re-layouts  3.65 us
  transfers between devices with their start and end apart: 6, of which 2 were waited for; matrix products, arithmetic and copies ran while one was open for 11% of the time, Pallas kernels for 0%

commit v1 on v0

--- a/solution.py
+++ b/solution.py
@@ -45,7 +45,9 @@
     spectrum = jnp.concatenate([real, imag], axis=0).astype(jnp.bfloat16)
     filtered = dot(backward, spectrum) + skip[None, :] * values.astype(jnp.float32)
     gated = (gates.astype(jnp.float32) * filtered).astype(jnp.bfloat16)
-    rows = lax.all_gather(gated, "chan", axis=1, tiled=True)
+    answer = jnp.stack([gated for _ in range(jax.lax.axis_size("chan"))])
+    top = jax.lax.all_to_all(answer, "chan", 0, 0)
+    rows = jnp.concatenate(top, axis=1)
     summed = dot(rows, columns).astype(jnp.bfloat16)
     return lax.all_to_all(summed, "chan", split_axis=0, concat_axis=1, tiled=True)
 

time: 167 us -> 122 us (0.73)
  the two profiles are of different devices: /device:TPU:1 before, /device:TPU:16 now
where the time goes in v1:
time: 122 us; the launch traced here: 121 us
  blocking collectives  57 us (47%)
  waiting for transfers between devices  24.5 us (20%)
  between operations  13.6 us (11%)
  starting transfers between devices  13.3 us (11%)
  matrix products  8.48 us (7%)
  local copies, waits for them, and re-layouts  4.42 us (4%)
    all_to_all x1, blocking collectives, body(): top = jax.lax.all_to_all(answer, 'chan', 0, 0)  31.5 us
    all_gather x1, waiting for transfers between devices, body(): columns = lax.all_gather(part, 'seq', axis=0, tiled=True)  21.2 us
    ppermute x4, starting transfers between devices, from_behind(): lax.ppermute(value, axis, [(source, source + steps) for source in range(c...  13.3 us
    all_to_all x1, blocking collectives, body(): lax.all_to_all(summed, 'chan', split_axis=0, concat_axis=1, tiled=True)  13.3 us
    all_to_all x1, blocking collectives, body(): lax.all_to_all(out_weight, 'chan', split_axis=1, concat_axis=0, tiled=True)  12.2 us
    dot_general x15, matrix products, dot(): return jnp.dot(a, b, preferred_element_type=jnp.float32)  8.48 us
    ppermute x4, waiting for transfers between devices, from_behind(): lax.ppermute(value, axis, [(source, source + steps) for source in range(c...  3.28 us
    unnamed x16, local copies, waits for them, and re-layouts  2.49 us
  transfers between devices with their start and end apart: 5, of which 3 were waited for; matrix products, arithmetic and copies ran while one was open for 6% of the time, Pallas kernels for 0%

profile of v1, /device:TPU:16, one launch (start us, length us, event | category | flops | bytes accessed | tf_op | source)
XLA Modules:
  0.0 121.3 jit_solution(3758610942815144316)
XLA Ops:
  6.5 1.1 copy.26
  7.6 12.2 %all_to_all.43 = bf16[32,8,512]{2,0,1:T(8,128)(2,1)} all-to-all(bf16[32,8,512]{2,0,1:T(8,128)(2,1)S(1)} %bitcast.49), channel_id=1, replica_groups=mesh['seq'=16,'chan'=8] {'chan'}, dimensions={1} | all-to-all | bytes 524288 | tf_op jit(solution)/shard_map/all_to_all | solution.py:33
  19.8 3.9 %collective-permute-start.1 = (bf16[256,512]{1,0:T(8,128)(2,1)}, bf16[256,512]{1,0:T(8,128)(2,1)S(1)}, u32[]{:S(2)}, u32[]{:S(2)}) collective-permute-start(bf16[256,512]{1,0:T(8,128)(2,1)} %param.7), channel_id=1, source_target_pairs={{0,16},{8,24},{16,32},{24,40},{32,48},{40,56},{48,64},{56,72},{64,... | collective-permute-start | bytes 786440 | tf_op jit(solution)/shard_map/ppermute | solution.py:20
  23.8 2.7 %collective-permute-start.2 = (bf16[256,512]{1,0:T(8,128)(2,1)}, bf16[256,512]{1,0:T(8,128)(2,1)S(1)}, u32[]{:S(2)}, u32[]{:S(2)}) collective-permute-start(bf16[256,512]{1,0:T(8,128)(2,1)} %param.7), channel_id=1, source_target_pairs={{0,24},{8,32},{16,40},{24,48},{32,56},{40,64},{48,72},{56,80},{64,... | collective-permute-start | bytes 786440 | tf_op jit(solution)/shard_map/ppermute | solution.py:20
  26.5 3.1 %collective-permute-start = (bf16[256,512]{1,0:T(8,128)(2,1)}, bf16[256,512]{1,0:T(8,128)(2,1)S(1)}, u32[]{:S(2)}, u32[]{:S(2)}) collective-permute-start(bf16[256,512]{1,0:T(8,128)(2,1)} %param.7), channel_id=1, source_target_pairs={{0,8},{8,16},{16,24},{24,32},{32,40},{40,48},{48,56},{56,64},{64,7... | collective-permute-start | bytes 786440 | tf_op jit(solution)/shard_map/ppermute | solution.py:20
  29.6 3.5 %collective-permute-start.3 = (bf16[256,512]{1,0:T(8,128)(2,1)}, bf16[256,512]{1,0:T(8,128)(2,1)S(1)}, u32[]{:S(2)}, u32[]{:S(2)}) collective-permute-start(bf16[256,512]{1,0:T(8,128)(2,1)} %param.7), channel_id=1, source_target_pairs={{0,32},{8,40},{16,48},{24,56},{32,64},{40,72},{48,80},{56,88},{64,... | collective-permute-start | bytes 786440 | tf_op jit(solution)/shard_map/ppermute | solution.py:20
  33.2 1.1 copy.20
  34.3 1.1 copy.19
  35.4 0.3 fusion.10
  35.7 0.3 fusion.4
  36.0 0.3 fusion.6
  36.3 0.3 fusion.8
  36.7 0.1 copy-done.2
  36.7 0.3 fusion.13
  37.0 1.6 %collective-permute-done = bf16[256,512]{1,0:T(8,128)(2,1)S(1)} collective-permute-done((bf16[256,512]{1,0:T(8,128)(2,1)}, bf16[256,512]{1,0:T(8,128)(2,1)S(1)}, u32[]{:S(2)}, u32[]{:S(2)}) %collective-permute-start) | collective-permute-done | bytes 262176 | tf_op jit(solution)/shard_map/ppermute | solution.py:20
  38.7 0.3 convolution_add_fusion.3
  39.0 0.3 fusion.14
  39.3 0.3 convolution_add_fusion.2
  39.6 0.3 fusion.15
  39.9 0.3 convolution_add_fusion.1
  40.2 0.3 fusion.16
  40.5 1.6 %collective-permute-done.3 = bf16[256,512]{1,0:T(8,128)(2,1)S(1)} collective-permute-done((bf16[256,512]{1,0:T(8,128)(2,1)}, bf16[256,512]{1,0:T(8,128)(2,1)S(1)}, u32[]{:S(2)}, u32[]{:S(2)}) %collective-permute-start.3) | collective-permute-done | bytes 262176 | tf_op jit(solution)/shard_map/ppermute | solution.py:20
  42.1 0.3 convolution_add_fusion
  42.4 0.8 fusion.12
  43.2 0.1 copy-done.4
  43.3 0.8 fusion.3
  44.1 0.1 stack.2
  44.3 31.5 %all_to_all.44 = bf16[8,256,512]{1,2,0:T(8,128)(2,1)S(1)} all-to-all(bf16[8,256,512]{1,2,0:T(8,128)(2,1)S(1)} %stack.2), channel_id=1, replica_groups=mesh['seq'=16,'chan'=8] {'chan'}, dimensions={0} | all-to-all | bytes 4194304 | tf_op jit(solution)/shard_map/all_to_all | solution.py:49
  75.8 21.2 %all-gather.2.cloned.1.call-done = bf16[4096,512]{1,0:T(8,128)(2,1)} async-done(((bf16[256,512]{1,0:T(8,128)(2,1)}), bf16[4096,512]{1,0:T(8,128)(2,1)}) %all-gather.2.cloned.1.call-update) | async-done | bytes 4194320 | tf_op jit(solution)/shard_map/all_gather | solution.py:34
  97.0 3.4 %convolution_convert_fusion = bf16[256,512]{1,0:T(8,128)(2,1)S(1)} fusion(bf16[256,4096]{0,1:T(8,128)(2,1)S(1)} %bitcast.46, bf16[4096,512]{1,0:T(8,128)(2,1)} %all-gather.2.cloned.1.call-done), kind=kOutput, calls=%fused_computation.9 | convolution fusion | flops 1073872896 | bytes 6553600 | tf_op jit(solution)/shard_map/dot_general | solution.py:24
  100.5 13.3 %all_to_all.45 = bf16[8,32,512]{2,1,0:T(8,128)(2,1)S(1)} all-to-all(bf16[8,32,512]{2,1,0:T(8,128)(2,1)S(1)} %bitcast.51), channel_id=1, replica_groups=mesh['seq'=16,'chan'=8] {'chan'}, dimensions={0} | all-to-all | bytes 524288 | tf_op jit(solution)/shard_map/all_to_all | solution.py:52
  113.8 0.7 copy.24
  (16 shorter events, 0.1 us)
Async XLA Ops:
  6.5 28.9 %copy-start = (bf16[512,256]{1,0:T(8,128)(2,1)S(1)}, bf16[512,256]{1,0:T(8,128)(2,1)}, u32[]{:S(2)}) copy-start(bf16[512,256]{1,0:T(8,128)(2,1)} %constant.7) | copy-start | bytes 786436
  6.5 28.9 %copy-start.3 = (bf16[1024,512]{1,0:T(8,128)(2,1)S(1)}, bf16[1024,512]{1,0:T(8,128)(2,1)}, u32[]{:S(2)}) copy-start(bf16[1024,512]{1,0:T(8,128)(2,1)} %param.9) | copy-start | bytes 3145732
  6.5 90.5 %all-gather.2.cloned.1.call-start = ((), (), s32[]{:S(2)}) async-start(), calls=%async_computation.3 | async-start | bytes 4456448 | tf_op jit(solution)/shard_map/all_gather | solution.py:34
  19.8 19.4 %collective-permute-start.1 = (bf16[256,512]{1,0:T(8,128)(2,1)}, bf16[256,512]{1,0:T(8,128)(2,1)S(1)}, u32[]{:S(2)}, u32[]{:S(2)}) collective-permute-start(bf16[256,512]{1,0:T(8,128)(2,1)} %param.7), channel_id=1, source_target_pairs={{0,16},{8,24},{16,32},{24,40},{32,48},{40,56},{48,64},{56,72},{64,... | collective-permute-start | bytes 786440 | tf_op jit(solution)/shard_map/ppermute | solution.py:20
  23.8 16.1 %collective-permute-start.2 = (bf16[256,512]{1,0:T(8,128)(2,1)}, bf16[256,512]{1,0:T(8,128)(2,1)S(1)}, u32[]{:S(2)}, u32[]{:S(2)}) collective-permute-start(bf16[256,512]{1,0:T(8,128)(2,1)} %param.7), channel_id=1, source_target_pairs={{0,24},{8,32},{16,40},{24,48},{32,56},{40,64},{48,72},{56,80},{64,... | collective-permute-start | bytes 786440 | tf_op jit(solution)/shard_map/ppermute | solution.py:20
  26.5 12.2 %collective-permute-start = (bf16[256,512]{1,0:T(8,128)(2,1)}, bf16[256,512]{1,0:T(8,128)(2,1)S(1)}, u32[]{:S(2)}, u32[]{:S(2)}) collective-permute-start(bf16[256,512]{1,0:T(8,128)(2,1)} %param.7), channel_id=1, source_target_pairs={{0,8},{8,16},{16,24},{24,32},{32,40},{40,48},{48,56},{56,64},{64,7... | collective-permute-start | bytes 786440 | tf_op jit(solution)/shard_map/ppermute | solution.py:20
  29.6 12.5 %collective-permute-start.3 = (bf16[256,512]{1,0:T(8,128)(2,1)}, bf16[256,512]{1,0:T(8,128)(2,1)S(1)}, u32[]{:S(2)}, u32[]{:S(2)}) collective-permute-start(bf16[256,512]{1,0:T(8,128)(2,1)} %param.7), channel_id=1, source_target_pairs={{0,32},{8,40},{16,48},{24,56},{32,64},{40,72},{48,80},{56,88},{64,... | collective-permute-start | bytes 786440 | tf_op jit(solution)/shard_map/ppermute | solution.py:20
  35.7 1.0 copy-start.1
  35.7 1.0 copy-start.2
  40.2 2.2 %copy-start.5 = (bf16[256,256]{1,0:T(8,128)(2,1)S(1)}, bf16[256,256]{1,0:T(8,128)(2,1)}, u32[]{:S(2)}) copy-start(bf16[256,256]{1,0:T(8,128)(2,1)} %constant.9) | copy-start | bytes 393220
  42.4 0.9 copy-start.4
  42.4 0.9 copy-start.6
Sparse Core Ops, SparseCore 0:
  20.0 77.0 all-gather.1
